TPU v7x, 256 devices: a whole 4x4x8 slice. The times are simulated.
256 devices in a mesh: row: 16 (over z, y_lo), col: 8 (over x, y_hi), rep: 2 (over core).
Axes of the slice: x: 4, y: 4 (y_hi: 2, y_lo: 2; y = y_hi * 2 + y_lo), z: 8, core: 2. Of those that a mesh axis runs over, the one named last changes fastest.
Arguments:
- activations: bfloat16 [2048, 7168], P(('col', 'rep'), 'row'), may hold values from -6 to 6
- out_grad: bfloat16 [2048, 7168], P(('col', 'rep'), 'row'), may hold values from -1.5 to 1.5
- up_codes: int32 [7168, 18432], P('row', 'col'), may hold values from 0 to 253
- up_scales: int32 [224, 18432], P('row', 'col'), may hold values from -15 to -12
- down_codes: int32 [18432, 7168], P('col', 'row'), may hold values from 0 to 253
- down_scales: int32 [576, 7168], P('col', 'row'), may hold values from -15 to -12
Outputs:
- layer_out: bfloat16 [2048, 7168], P(('col', 'rep'), 'row')
- in_grad: bfloat16 [2048, 7168], P(('col', 'rep'), 'row')
- up_grad: bfloat16 [7168, 18432], P('row', 'col')
- down_grad: bfloat16 [18432, 7168], P('col', 'row')
All inputs are finite; a program needn't handle non-finite values.
Results may differ from a plain program's by a relative error of at most 0.025.
Values may be sent and summed in bfloat16 or wider, within the bound.
A program may use at most 128 MiB of HBM per device.

v0:
```python
import jax
import jax.numpy as jnp
from jax import lax
from jax.sharding import PartitionSpec as P

BLOCK = 32


def decode(code_words, scale_exps, block_size):
    sign_bit = code_words // 127
    magnitude = code_words % 127
    exponent = magnitude // 8
    mantissa = magnitude % 8
    normal = exponent > 0
    rows_count = scale_exps.shape[0]
    cols_count = scale_exps.shape[1]
    scale_grid = jnp.broadcast_to(
        scale_exps[:, None, :], (rows_count, block_size, cols_count)
    ).reshape(code_words.shape)
    shift_count = -(jnp.where(normal, exponent - 10, -9) + scale_grid)
    factor = jnp.ones(code_words.shape, jnp.float32)
    halvings = (0.5, 0.25, 0.0625, 0.00390625, 1.52587890625e-05)
    for position in range(5):
        chosen = shift_count // 2**position % 2 == 1
        factor = factor * jnp.where(chosen, jnp.float32(halvings[position]), jnp.float32(1.0))
    mant_value = jnp.where(normal, mantissa + 8, mantissa).astype(jnp.float32)
    signed = (1 - 2 * sign_bit).astype(jnp.float32)
    return (mant_value * factor * signed).astype(jnp.bfloat16)


def gelu_parts(pre_total):
    cdf_value = 0.5 * (1.0 + jax.scipy.special.erf(pre_total * 0.7071067811865476))
    density = jnp.exp(-0.5 * pre_total * pre_total) * 0.3989422804014327
    return (pre_total * cdf_value, cdf_value + pre_total * density)


def replica_total(partial_value):
    return lax.psum(partial_value.astype(jnp.bfloat16), "rep")


def body(activations, out_grad, up_codes, up_scales, down_codes, down_scales):
    contract_last = (((1,), (1,)), ((), ()))
    contract_first = (((0,), (0,)), ((), ()))
    up_weight = decode(up_codes, up_scales, BLOCK)
    down_weight = decode(down_codes, down_scales, BLOCK)
    acts_all, grads_all = (
        lax.all_gather(activations, "col", axis=0, tiled=True),
        lax.all_gather(out_grad, "col", axis=0, tiled=True),
    )
    pre_part = jnp.dot(acts_all, up_weight, preferred_element_type=jnp.float32)
    back_part = lax.dot_general(
        grads_all, down_weight, contract_last, preferred_element_type=jnp.float32
    )
    pre_total, back_total = (
        lax.psum(pre_part.astype(jnp.bfloat16), "row").astype(jnp.float32),
        lax.psum(back_part.astype(jnp.bfloat16), "row").astype(jnp.float32),
    )
    activated, gelu_slope = gelu_parts(pre_total)
    gelu_out = activated.astype(jnp.bfloat16)
    hidden_grad = (back_total * gelu_slope).astype(jnp.bfloat16)
    down_grad = replica_total(
        lax.dot_general(gelu_out, grads_all, contract_first, preferred_element_type=jnp.float32)
    )
    out_part = jnp.dot(gelu_out, down_weight, preferred_element_type=jnp.float32)
    in_part = lax.dot_general(
        hidden_grad, up_weight, contract_last, preferred_element_type=jnp.float32
    )
    out_sum, in_sum = (
        lax.psum_scatter(
            out_part.astype(jnp.bfloat16), "col", scatter_dimension=0, tiled=True
        ).astype(jnp.float32),
        lax.psum_scatter(
            in_part.astype(jnp.bfloat16), "col", scatter_dimension=0, tiled=True
        ).astype(jnp.float32),
    )
    layer_out = out_sum.astype(jnp.bfloat16)
    in_grad = in_sum.astype(jnp.bfloat16)
    up_grad = replica_total(
        lax.dot_general(acts_all, hidden_grad, contract_first, preferred_element_type=jnp.float32)
    )
    return (layer_out, in_grad, up_grad, down_grad)


def solution(mesh):
    placed = (
        P(("col", "rep"), "row"),
        P(("col", "rep"), "row"),
        P("row", "col"),
        P("row", "col"),
        P("col", "row"),
        P("col", "row"),
    )
    return jax.shard_map(
        body,
        mesh=mesh,
        in_specs=placed,
        out_specs=(
            P(("col", "rep"), "row"),
            P(("col", "rep"), "row"),
            P("row", "col"),
            P("col", "row"),
        ),
        check_vma=False,
    )
```

profile of v0, /device:TPU:1, one launch (start us, length us, event | category | flops | bytes accessed | tf_op | source)
XLA Modules:
  0.0 786.9 jit_solution(16063781059810175605)
XLA Ops:
  7.2 0.0 all-reduce.5.cloned.1.call-start
  7.2 31.7 %all_gather.6 = bf16[1024,448]{0,1:T(8,128)(2,1)S(1)} all-gather(bf16[128,448]{0,1:T(8,128)(2,1)} %param.6), channel_id=1, replica_groups=mesh['row'=16,'col'=8,'rep'=2] {'col'}, dimensions={0}, use_global_device_ids=true | all-gather | bytes 1032192 | tf_op jit(solution)/shard_map/all_gather | solution.py:47
  38.9 0.0 copy-start.6
  38.9 28.3 %all_gather.7 = bf16[1024,448]{0,1:T(8,128)(2,1)S(1)} all-gather(bf16[128,448]{0,1:T(8,128)(2,1)} %param.7), channel_id=1, replica_groups=mesh['row'=16,'col'=8,'rep'=2] {'col'}, dimensions={0}, use_global_device_ids=true | all-gather | bytes 1032192 | tf_op jit(solution)/shard_map/all_gather | solution.py:48
  67.2 0.0 copy-start.1
  67.2 0.0 copy-start.7
  67.2 6.2 copy.14
  73.4 0.0 copy-done.7
  73.4 0.0 slice-start
  73.4 26.8 %fusion.42 = bf16[448,2304]{1,0:T(8,128)(2,1)S(1)} fusion(s32[448,2304]{1,0:T(8,128)} %param.8, s32[14,2304]{1,0:T(8,128)S(1)} %copy-done.7), kind=kLoop, calls=%fused_computation.127 | loop fusion | flops 155860992 | bytes 6322176 | tf_op jit(solution)/shard_map/convert_element_type | solution.py:28
  100.3 0.0 copy-done.6
  100.3 0.0 copy-start.3
  100.3 0.0 slice-start.1
  100.3 0.0 copy-start.8
  100.3 4.3 fusion.9
  104.6 0.0 copy-done.3
  104.6 0.0 slice-done
  104.6 0.0 slice-done.1
  104.6 0.0 copy-done.8
  104.6 29.5 %fusion.15 = bf16[2304,448]{1,0:T(8,128)(2,1)S(1)} fusion(s32[2304,448]{1,0:T(8,128)S(1)} %bitcast.27, s32[72,448]{1,0:T(8,128)S(1)} %copy-done.8), kind=kLoop, calls=%fused_computation.94 | loop fusion | flops 155860992 | bytes 6322176 | tf_op jit(solution)/shard_map/convert_element_type | solution.py:28
  134.1 0.0 copy-done.1
  134.1 4.3 fusion.10
  138.4 0.0 all-reduce.5.cloned.1.call-update
  138.4 0.0 reduce-scatter.9.cloned.1.call-start
  138.5 419.3 %all-reduce.5.cloned.1.call-done = (bf16[1024,2304]{0,1:T(8,128)(2,1)}, bf16[1024,2304]{0,1:T(8,128)(2,1)}) async-done(((bf16[1024,2304]{0,1:T(8,128)(2,1)}, bf16[1024,2304]{0,1:T(8,128)(2,1)}), (bf16[1024,2304]{0,1:T(8,128)(2,1)}, bf16[1024,2304]{0,1:T(8,128)(2,1)})) %all-reduce.5.cloned.1.call-update) | async-done | bytes 9437200 | tf_op jit(solution)/shard_map/psum | solution.py:55
  557.8 0.0 copy-start.4
  557.8 11.3 %fusion.8 = (bf16[1024,2304]{0,1:T(8,128)(2,1)S(1)}, f32[1024,2304]{0,1:T(8,128)}) fusion(bf16[1024,2304]{0,1:T(8,128)(2,1)} %get-tuple-element.4, bf16[1024,2304]{0,1:T(8,128)(2,1)} %get-tuple-element.5), kind=kLoop, calls=%fused_computation.13 | loop fusion | flops 28311552 | bytes 23592960 | tf_op jit(solution)/shard_map/convert_element_type | solution.py:60
  569.1 0.0 copy-start
  569.1 2.1 copy-done
  571.3 0.0 copy-done.4
  571.3 2.3 convolution_convert_fusion.4
  573.6 1.3 copy.19
  574.9 0.0 reduce-scatter.9.cloned.1.call-update
  574.9 0.2 reduce-scatter.7.cloned.1.call-start
  575.1 7.4 convolution_convert_fusion.5
  582.5 1.3 copy.17
  583.8 0.0 reduce-scatter.7.cloned.1.call-update
  583.8 0.0 copy-start.2
  583.8 0.0 all-reduce.7.cloned.1.call-start
  583.9 6.3 fusion.65
  590.2 0.0 copy-done.2
  590.2 8.7 %convolution_convert_fusion.2 = bf16[2304,448]{0,1:T(8,128)(2,1)} fusion(bf16[1024,448]{0,1:T(8,128)(2,1)S(1)} %copy-done.2, f32[1024,2304]{0,1:T(8,128)} %get-tuple-element.9, bf16[1024,2304]{0,1:T(8,128)(2,1)} %get-tuple-element.4), kind=kOutput, calls=%fused_computation.121 | convolution fusion | flops 2122039296 | bytes 17137664 | tf_op jit(solution)/shard_map/dot_general | solution.py:62
  598.9 0.0 all-reduce.7.cloned.1.call-update
  599.0 52.1 %reduce-scatter.9.cloned.1.call-done = bf16[128,448]{1,0:T(8,128)(2,1)} async-done(((bf16[1024,448]{1,0:T(8,128)(2,1)}), bf16[128,448]{1,0:T(8,128)(2,1)}) %reduce-scatter.9.cloned.1.call-update) | async-done | bytes 114704
  651.1 1.7 copy.20
  652.7 78.9 %reduce-scatter.7.cloned.1.call-done = bf16[128,448]{1,0:T(8,128)(2,1)} async-done(((bf16[1024,448]{1,0:T(8,128)(2,1)}), bf16[128,448]{1,0:T(8,128)(2,1)}) %reduce-scatter.7.cloned.1.call-update) | async-done | bytes 114704
  731.6 1.7 copy.18
  733.3 42.6 %all-reduce.7.cloned.1.call-done = (bf16[448,2304]{1,0:T(8,128)(2,1)}, bf16[2304,448]{0,1:T(8,128)(2,1)}) async-done(((bf16[448,2304]{1,0:T(8,128)(2,1)}, bf16[2304,448]{0,1:T(8,128)(2,1)}), (bf16[448,2304]{1,0:T(8,128)(2,1)}, bf16[2304,448]{0,1:T(8,128)(2,1)})) %all-reduce.7.cloned.1.call-update) | async-done | bytes 4128784 | tf_op jit(solution)/shard_map/psum | solution.py:38
  775.9 0.0 copy-start.5
  775.9 3.2 copy.25
  779.1 0.0 copy-done.5
  779.1 1.3 copy.26
  (1 shorter events, 0.0 us)
Async XLA Ops:
  7.2 550.6 %all-reduce.5.cloned.1.call-start = ((), (), s32[]{:S(2)}) async-start(), calls=%async_computation.4 | async-start | bytes 18874368 | tf_op jit(solution)/shard_map/psum | solution.py:55
  38.9 61.4 %copy-start.6 = (bf16[1024,448]{0,1:T(8,128)(2,1)}, bf16[1024,448]{0,1:T(8,128)(2,1)S(1)}, u32[]{:S(2)}) copy-start(bf16[1024,448]{0,1:T(8,128)(2,1)S(1)} %all_gather.6) | copy-start | bytes 2752516
  67.2 66.9 %copy-start.1 = (bf16[1024,448]{0,1:T(8,128)(2,1)}, bf16[1024,448]{0,1:T(8,128)(2,1)S(1)}, u32[]{:S(2)}) copy-start(bf16[1024,448]{0,1:T(8,128)(2,1)S(1)} %all_gather.7) | copy-start | bytes 2752516
  67.2 6.2 copy-start.7
  73.4 31.2 %slice-start = ((s8[4718592]{0:T(1024)(128)(4,1)}), s8[4194304]{0:T(1024)(128)(4,1)S(1)}, s32[]{:S(2)}) async-start(s8[4718592]{0:T(1024)(128)(4,1)} %bitcast.26), calls=%async_computation.6 | async-start | bytes 8388608
  100.3 4.3 copy-start.3
  100.3 4.3 slice-start.1
  100.3 4.3 copy-start.8
  138.4 512.6 %reduce-scatter.9.cloned.1.call-start = ((), (), s32[]{:S(2)}) async-start(), calls=%async_computation.3 | async-start | bytes 1179648
  557.8 13.4 %copy-start.4 = (bf16[448,2304]{1,0:T(8,128)(2,1)S(1)}, bf16[448,2304]{1,0:T(8,128)(2,1)}, u32[]{:S(2)}) copy-start(bf16[448,2304]{1,0:T(8,128)(2,1)} %copy-done.3) | copy-start | bytes 6193156
  569.1 2.1 copy-start
  574.9 156.8 %reduce-scatter.7.cloned.1.call-start = ((), (), s32[]{:S(2)}) async-start(), calls=%async_computation.2 | async-start | bytes 1179648
  583.8 6.4 copy-start.2
  583.8 192.0 %all-reduce.7.cloned.1.call-start = ((), (), s32[]{:S(2)}) async-start(), calls=%async_computation.5 | async-start | bytes 8257536 | tf_op jit(solution)/shard_map/psum | solution.py:38
  775.9 3.2 copy-start.5
Sparse Core Ops, SparseCore 0:
  138.6 419.2 all-reduce.4
  575.0 76.0 reduce-scatter.8
  655.5 76.0 reduce-scatter.6
  734.9 40.9 all-reduce.6
where the time goes:
time: 787 us
  waiting for transfers between devices  593 us (75%)
  other arithmetic  67.6 us (9%)
  blocking collectives  60 us (8%)
  matrix products  33.3 us (4%)
  local copies, waits for them, and re-layouts  18.8 us (2%)
  between operations  13.9 us (2%)
    psum x1, waiting for transfers between devices, body(): lax.psum(pre_part.astype(jnp.bfloat16), 'row').astype(jnp.float32)  419 us
    unnamed x6, waiting for transfers between devices  131 us
    convert_element_type x2, other arithmetic, decode(): return (mant_value * factor * signed).astype(jnp.bfloat16)  56.3 us
    psum x1, waiting for transfers between devices, replica_total(): return lax.psum(partial_value.astype(jnp.bfloat16), 'rep')  42.6 us
    all_gather x1, blocking collectives, body(): lax.all_gather(activations, 'col', axis=0, tiled=True)  31.7 us
    all_gather x1, blocking collectives, body(): lax.all_gather(out_grad, 'col', axis=0, tiled=True)  28.3 us
    unnamed x29, local copies, waits for them, and re-layouts  18.8 us
  transfers between devices with their start and end apart: 4, of which 4 were waited for; matrix products, arithmetic and copies ran while one was open for 3% of the time, Pallas kernels for 0%

commit v1 on v0

--- a/solution.py
+++ b/solution.py
@@ -4,6 +4,15 @@
 from jax.sharding import PartitionSpec as P
 
 BLOCK = 32
+number_leaves = lambda out_dim, frame_in: jnp.concatenate(
+    lax.all_to_all(
+        jnp.stack([frame_in for _ in range(lax.axis_size("col"))], 0),
+        axis_name="col",
+        split_axis=0,
+        concat_axis=0,
+    ),
+    out_dim,
+)
 
 
 def decode(code_words, scale_exps, block_size):
@@ -44,7 +53,7 @@
     up_weight = decode(up_codes, up_scales, BLOCK)
     down_weight = decode(down_codes, down_scales, BLOCK)
     acts_all, grads_all = (
-        lax.all_gather(activations, "col", axis=0, tiled=True),
+        number_leaves(0, activations),
         lax.all_gather(out_grad, "col", axis=0, tiled=True),
     )
     pre_part = jnp.dot(acts_all, up_weight, preferred_element_type=jnp.float32)

time: 787 us -> 767 us (0.975)
  blocking collectives: 60 us -> 30.5 us
    all_gather x1 -> x0, blocking collectives: 31.7 us -> none  [body(): lax.all_gather(activations, 'col', axis=0, tiled=True)]
    unnamed x29 -> x27, local copies, waits for them, and re-layouts: 18.8 us -> 19.4 us
  transfers between devices with their start and end apart: 4 -> 5, of which waited for: 4 -> 4; matrix products, arithmetic and copies ran while one was open for 3% -> 12% of each run, Pallas kernels for 0% -> 0%
where the time goes in v1:
time: 767 us; the launch traced here: 766 us
  waiting for transfers between devices  589 us (77%)
  other arithmetic  68.3 us (9%)
  matrix products  35.2 us (5%)
  blocking collectives  30.5 us (4%)
  local copies, waits for them, and re-layouts  21.3 us (3%)
  between operations  13.8 us (2%)
  starting transfers between devices  7.83 us (1%)
    psum x1, waiting for transfers between devices, body(): lax.psum(pre_part.astype(jnp.bfloat16), 'row').astype(jnp.float32)  416 us
    unnamed x6, waiting for transfers between devices  131 us
    convert_element_type x2, other arithmetic, decode(): return (mant_value * factor * signed).astype(jnp.bfloat16)  57 us
    psum x1, waiting for transfers between devices, replica_total(): return lax.psum(partial_value.astype(jnp.bfloat16), 'rep')  42.6 us
    all_gather x1, blocking collectives, body(): lax.all_gather(out_grad, 'col', axis=0, tiled=True)  30.5 us
    unnamed x27, local copies, waits for them, and re-layouts  19.4 us
  transfers between devices with their start and end apart: 5, of which 4 were waited for; matrix products, arithmetic and copies ran while one was open for 12% of the time, Pallas kernels for 0%

profile of v1, /device:TPU:1, one launch (start us, length us, event | category | flops | bytes accessed | tf_op | source)
XLA Modules:
  0.0 766.5 jit_solution(2980425912790366377)
XLA Ops:
  7.2 1.9 stack.2
  9.1 7.5 all-to-all-start
  16.6 0.0 copy-start.7
  16.6 0.0 all-reduce.5.cloned.1.call-start
  16.6 5.8 copy.20
  22.5 0.0 copy-done.7
  22.5 0.0 copy-start
  22.5 0.0 copy-start.8
  22.5 27.5 %fusion.42 = bf16[448,2304]{1,0:T(8,128)(2,1)} fusion(s32[448,2304]{1,0:T(8,128)} %param.8, s32[14,2304]{1,0:T(8,128)S(1)} %copy-done.7), kind=kLoop, calls=%fused_computation.127 | loop fusion | flops 155860992 | bytes 6322176 | tf_op jit(solution)/shard_map/convert_element_type | solution.py:37
  50.0 0.0 copy-done
  50.0 0.0 copy-done.8
  50.0 0.0 copy-start.9
  50.0 29.5 %fusion.15 = bf16[2304,448]{1,0:T(8,128)(2,1)S(1)} fusion(s32[2304,448]{1,0:T(8,128)S(1)} %copy-done, s32[72,448]{1,0:T(8,128)S(1)} %copy-done.8), kind=kLoop, calls=%fused_computation.94 | loop fusion | flops 155860992 | bytes 6322176 | tf_op jit(solution)/shard_map/convert_element_type | solution.py:37
  79.5 0.0 copy-done.9
  79.5 30.5 %all_gather.3 = bf16[1024,448]{0,1:T(8,128)(2,1)S(1)} all-gather(bf16[128,448]{0,1:T(8,128)(2,1)S(1)} %copy-done.9), channel_id=1, replica_groups=mesh['row'=16,'col'=8,'rep'=2] {'col'}, dimensions={0}, use_global_device_ids=true | all-gather | bytes 1032192 | tf_op jit(solution)/shard_map/all_gather | solution.py:57
  110.1 0.0 copy-start.2
  110.1 0.9 copy-done.2
  111.0 4.3 fusion.10
  115.3 0.0 all-to-all-done
  115.3 0.0 copy-start.6
  115.3 6.3 fusion.9
  121.5 0.0 copy-done.6
  121.5 0.0 all-reduce.5.cloned.1.call-update
  121.6 0.0 reduce-scatter.9.cloned.1.call-start
  121.6 415.7 %all-reduce.5.cloned.1.call-done = (bf16[1024,2304]{0,1:T(8,128)(2,1)}, bf16[1024,2304]{0,1:T(8,128)(2,1)}) async-done(((bf16[1024,2304]{0,1:T(8,128)(2,1)}, bf16[1024,2304]{0,1:T(8,128)(2,1)}), (bf16[1024,2304]{0,1:T(8,128)(2,1)}, bf16[1024,2304]{0,1:T(8,128)(2,1)})) %all-reduce.5.cloned.1.call-update) | async-done | bytes 9437200 | tf_op jit(solution)/shard_map/psum | solution.py:64
  537.3 0.0 copy-start.4
  537.3 11.3 %fusion.8 = (bf16[1024,2304]{0,1:T(8,128)(2,1)S(1)}, f32[1024,2304]{0,1:T(8,128)}) fusion(bf16[1024,2304]{0,1:T(8,128)(2,1)} %get-tuple-element.4, bf16[1024,2304]{0,1:T(8,128)(2,1)} %get-tuple-element.5), kind=kLoop, calls=%fused_computation.13 | loop fusion | flops 28311552 | bytes 23592960 | tf_op jit(solution)/shard_map/convert_element_type | solution.py:69
  548.7 0.0 copy-start.1
  548.7 2.1 copy-done.1
  550.8 0.0 copy-done.4
  550.8 2.3 convolution_convert_fusion.4
  553.1 1.3 copy.25
  554.4 0.0 reduce-scatter.9.cloned.1.call-update
  554.4 0.2 reduce-scatter.7.cloned.1.call-start
  554.7 7.4 convolution_convert_fusion.5
  562.1 1.3 copy.23
  563.4 0.0 reduce-scatter.7.cloned.1.call-update
  563.4 0.0 copy-start.3
  563.4 0.0 all-reduce.7.cloned.1.call-start
  563.5 6.3 fusion.65
  569.8 0.0 copy-done.3
  569.8 8.7 %convolution_convert_fusion.2 = bf16[2304,448]{0,1:T(8,128)(2,1)} fusion(bf16[1024,448]{0,1:T(8,128)(2,1)S(1)} %copy-done.3, f32[1024,2304]{0,1:T(8,128)} %get-tuple-element.9, bf16[1024,2304]{0,1:T(8,128)(2,1)} %get-tuple-element.4), kind=kOutput, calls=%fused_computation.121 | convolution fusion | flops 2122039296 | bytes 17137664 | tf_op jit(solution)/shard_map/dot_general | solution.py:71
  578.5 0.0 all-reduce.7.cloned.1.call-update
  578.5 52.1 %reduce-scatter.9.cloned.1.call-done = bf16[128,448]{1,0:T(8,128)(2,1)} async-done(((bf16[1024,448]{1,0:T(8,128)(2,1)}), bf16[128,448]{1,0:T(8,128)(2,1)}) %reduce-scatter.9.cloned.1.call-update) | async-done | bytes 114704
  630.6 1.7 copy.26
  632.3 78.9 %reduce-scatter.7.cloned.1.call-done = bf16[128,448]{1,0:T(8,128)(2,1)} async-done(((bf16[1024,448]{1,0:T(8,128)(2,1)}), bf16[128,448]{1,0:T(8,128)(2,1)}) %reduce-scatter.7.cloned.1.call-update) | async-done | bytes 114704
  711.2 1.7 copy.24
  712.9 42.6 %all-reduce.7.cloned.1.call-done = (bf16[448,2304]{1,0:T(8,128)(2,1)}, bf16[2304,448]{0,1:T(8,128)(2,1)}) async-done(((bf16[448,2304]{1,0:T(8,128)(2,1)}, bf16[2304,448]{0,1:T(8,128)(2,1)}), (bf16[448,2304]{1,0:T(8,128)(2,1)}, bf16[2304,448]{0,1:T(8,128)(2,1)})) %all-reduce.7.cloned.1.call-update) | async-done | bytes 4128784 | tf_op jit(solution)/shard_map/psum | solution.py:47
  755.5 0.0 copy-start.5
  755.5 3.2 copy.40
  758.6 0.0 copy-done.5
  758.6 1.3 copy.41
Async XLA Ops:
  9.1 106.2 %all-to-all-start = ((bf16[8,128,448]{1,2,0:T(8,128)(2,1)}), bf16[8,128,448]{1,2,0:T(8,128)(2,1)S(1)}, u32[]{:S(2)}, u32[]{:S(2)}) async-start(bf16[8,128,448]{1,2,0:T(8,128)(2,1)} %stack.2), calls=%async_computation | async-start | bytes 1835008 | tf_op jit(solution)/shard_map/all_to_all | solution.py:8
  16.6 5.9 copy-start.7
  16.6 520.8 %all-reduce.5.cloned.1.call-start = ((), (), s32[]{:S(2)}) async-start(), calls=%async_computation.5 | async-start | bytes 18874368 | tf_op jit(solution)/shard_map/psum | solution.py:64
  22.5 27.5 %copy-start = (s32[2304,448]{1,0:T(8,128)S(1)}, s32[2304,448]{1,0:T(8,128)}, u32[]{:S(2)}) copy-start(s32[2304,448]{1,0:T(8,128)} %copy.20) | copy-start | bytes 12386308
  22.5 27.5 %copy-start.8 = (s32[72,448]{1,0:T(8,128)S(1)}, s32[72,448]{1,0:T(8,128)}, u32[]{:S(2)}) copy-start(s32[72,448]{1,0:T(8,128)} %param.11) | copy-start | bytes 387076
  50.0 29.5 %copy-start.9 = (bf16[128,448]{0,1:T(8,128)(2,1)S(1)}, bf16[128,448]{0,1:T(8,128)(2,1)}, u32[]{:S(2)}) copy-start(bf16[128,448]{0,1:T(8,128)(2,1)} %param.7) | copy-start | bytes 344068
  110.1 0.9 copy-start.2
  115.3 6.3 copy-start.6
  121.6 509.1 %reduce-scatter.9.cloned.1.call-start = ((), (), s32[]{:S(2)}) async-start(), calls=%async_computation.4 | async-start | bytes 1179648
  537.3 13.5 %copy-start.4 = (bf16[448,2304]{1,0:T(8,128)(2,1)S(1)}, bf16[448,2304]{1,0:T(8,128)(2,1)}, u32[]{:S(2)}) copy-start(bf16[448,2304]{1,0:T(8,128)(2,1)} %fusion.42) | copy-start | bytes 6193156
  548.7 2.1 copy-start.1
  554.4 156.8 %reduce-scatter.7.cloned.1.call-start = ((), (), s32[]{:S(2)}) async-start(), calls=%async_computation.3 | async-start | bytes 1179648
  563.4 6.4 copy-start.3
  563.4 192.1 %all-reduce.7.cloned.1.call-start = ((), (), s32[]{:S(2)}) async-start(), calls=%async_computation.6 | async-start | bytes 8257536 | tf_op jit(solution)/shard_map/psum | solution.py:47
  755.5 3.2 copy-start.5
Sparse Core Ops, SparseCore 0:
  121.7 415.6 all-reduce.4
  554.6 76.0 reduce-scatter.8
  635.1 76.0 reduce-scatter.6
  714.5 40.9 all-reduce.6
